TPU v7x, 512 devices: a whole 4x4x16 slice. The times are simulated.
512 devices in a mesh: grp: 16 (over y, x), dev: 32 (over z, core).
Axes of the slice: x: 4, y: 4, z: 16, core: 2. Of those that a mesh axis runs over, the one named last changes fastest.
Arguments:
- points: float32 [3, 524288], P(None, ('grp', 'dev')), may hold values from 0 to 2
- charges: float32 [16, 524288], P(None, ('grp', 'dev')), may hold values from -6 to 6
- morton: int32 [524288], P(('grp', 'dev')), may hold values from 0 to 1023, as said below
- neighbours: int32 [2048, 8], P(('grp', 'dev')), may hold values from 0 to 2047, as said below
- counts: int32 [2048], P(('grp', 'dev')), may hold values from 1 to 8
- skel_leaf: float32 [3, 524288], P(None, ('grp', 'dev')), may hold values from 0 to 2
- skel_block: float32 [3, 131072], P(None, ('grp', 'dev')), may hold values from 0 to 2
- skel_group: float32 [3, 4096], replicated, may hold values from 0 to 2
Outputs:
- potential: float32 [16, 524288], P(None, ('grp', 'dev'))
Inputs may be any that keep to these rules, and one draw needn't show every extreme that they name: `morton`: each aligned run of 1024 entries is a permutation of 0 to 1023. `neighbours`: entry [q, k] is a leaf other than q, at most 4 leaves away from q; only slots k < counts[q] are used.
All inputs are finite; a program needn't handle non-finite values.
Results may differ from a plain program's by a relative error of at most 0.0003.
Values sent between devices are 32-bit elements; how exact they have to be, the bound alone decides.
No kernel may reach another device: no remote copies, remote signals or barrier semaphores. Data moves between devices by JAX's collectives and lax.ppermute only.
A program may use at most 64 MiB of HBM per device.

v0:
```python
import math
import jax
import jax.numpy as jnp
from jax import lax
from jax.sharding import PartitionSpec as P

width_sq = 0.1
gain_factor = 5.0


def extended_2(cells, sides, width):
    for axis, dim in sides:
        count = lax.axis_size(axis)
        ends = count - 1
        head = lax.slice_in_dim(cells, 0, width, axis=dim)
        tail = lax.slice_in_dim(cells, cells.shape[dim] - width, cells.shape[dim], axis=dim)
        cells = jnp.concatenate(
            [
                lax.ppermute(tail, axis, [(i, (i + 1) % count) for i in range(ends)]),
                cells,
                lax.ppermute(head, axis, [((i + 1) % count, i) for i in range(ends)]),
            ],
            axis=dim,
        )
    return cells


def kernel_tile(source, target):
    distance = (source[0][:, None] - target[0][None, :]) ** 2
    distance = distance + (source[1][:, None] - target[1][None, :]) ** 2
    distance = distance + (source[2][:, None] - target[2][None, :]) ** 2
    return jnp.exp(-distance / width_sq)


def translate(values, source, target, term_count):
    product = jnp.dot(
        values,
        kernel_tile(source, target),
        precision=lax.Precision.HIGHEST,
        preferred_element_type=jnp.float32,
    )
    return gain_factor / math.sqrt(term_count) * product


def far_sum(running, weights, skeleton, target, own_member, skel_rank, term_count):
    span_cols = weights.shape[1]
    block_cols = min(skel_rank, span_cols)

    def one_block(block_index, partial_value):
        column = block_index * block_cols
        piece_w = lax.dynamic_slice_in_dim(weights, column, block_cols, 1)
        piece_s = lax.dynamic_slice_in_dim(skeleton, column, block_cols, 1)
        member = column // skel_rank
        keep_mask = jnp.where(member == own_member, 0.0, 1.0)
        return partial_value + keep_mask * translate(piece_w, piece_s, target, term_count)

    return lax.fori_loop(0, span_cols // block_cols, one_block, running)


def body(points, charges, morton, neighbours, counts, skel_leaf, skel_block, skel_group):
    n_groups = lax.axis_size("grp")
    n_blocks = lax.axis_size("dev")
    vectors, block_pts = charges.shape
    leaf_count = counts.shape[0]
    leaf_size = block_pts // leaf_count
    skel_rank = skel_block.shape[1]
    slot_total = neighbours.shape[1]
    group_id = lax.axis_index("grp")
    member_id = lax.axis_index("dev")
    block_id = group_id * n_blocks + member_id
    sorted_pts = jnp.take(points, morton, axis=1)
    sorted_chg = jnp.take(charges, morton, axis=1)
    leaf_pts = sorted_pts.reshape(3, leaf_count, leaf_size).transpose(1, 0, 2)
    leaf_chg = sorted_chg.reshape(vectors, leaf_count, leaf_size).transpose(1, 0, 2)
    leaf_skel = skel_leaf.reshape(3, leaf_count, skel_rank).transpose(1, 0, 2)
    leaf_weights = lax.map(
        lambda inputs: translate(inputs[0], inputs[1], inputs[2], leaf_size),
        (leaf_chg, leaf_pts, leaf_skel),
    )
    lifted = lax.map(
        lambda inputs: translate(inputs[0], inputs[1], skel_block, leaf_count * skel_rank),
        (leaf_weights, leaf_skel),
    )
    block_weights = jnp.sum(lifted, axis=0)
    own_group = lax.dynamic_slice_in_dim(skel_group, group_id * skel_rank, skel_rank, 1)
    raised = translate(block_weights, skel_block, own_group, n_blocks * skel_rank)
    empty = jnp.zeros((vectors, skel_rank), jnp.float32)
    group_terms = (n_groups - 1) * skel_rank
    group_weights = lax.psum(raised, "dev")
    group_field = far_sum(
        empty,
        lax.all_gather(group_weights, "grp", axis=1, tiled=True),
        skel_group,
        own_group,
        group_id,
        skel_rank,
        group_terms,
    )
    peer_field = far_sum(
        empty,
        lax.all_gather(block_weights, "dev", axis=1, tiled=True),
        lax.all_gather(skel_block, "dev", axis=1, tiled=True),
        skel_block,
        member_id,
        skel_rank,
        (n_blocks - 1) * skel_rank,
    )
    block_field = peer_field + translate(group_field, own_group, skel_block, skel_rank)
    leaf_field = lax.map(
        lambda target: translate(block_field, skel_block, target, skel_rank), leaf_skel
    )
    stacked = jnp.concatenate([sorted_pts, sorted_chg], axis=0)
    extended = extended_2(stacked, ((("grp", "dev"), 1),), block_pts)
    ext_leaves = extended.reshape(3 + vectors, 3 * leaf_count, leaf_size).transpose(1, 0, 2)
    first_leaf = block_id * leaf_count - leaf_count

    def near_leaf(inputs):
        own_pts, own_chg, own_field, own_skel, row_nbr, row_count = inputs
        direct = translate(own_chg, own_pts, own_pts, leaf_size)
        direct = direct + translate(own_field, own_skel, own_pts, skel_rank)

        def one_slot(slot_index, running):
            source = lax.dynamic_index_in_dim(
                ext_leaves, row_nbr[slot_index] - first_leaf, 0, keepdims=False
            )
            tile_term = translate(source[3:], source[:3], own_pts, leaf_size)
            return running + jnp.where(slot_index < row_count, tile_term, jnp.zeros_like(tile_term))

        return lax.fori_loop(0, slot_total, one_slot, direct)

    potential = lax.map(near_leaf, (leaf_pts, leaf_chg, leaf_field, leaf_skel, neighbours, counts))
    return potential.transpose(1, 0, 2).reshape(vectors, block_pts)


def solution(mesh):
    return jax.shard_map(
        body,
        mesh=mesh,
        in_specs=(
            P(None, ("grp", "dev")),
            P(None, ("grp", "dev")),
            P(("grp", "dev")),
            P(("grp", "dev"), None),
            P(("grp", "dev")),
            P(None, ("grp", "dev")),
            P(None, ("grp", "dev")),
            P(),
        ),
        out_specs=P(None, ("grp", "dev")),
        check_vma=False,
    )
```

profile of v0, /device:TPU:8, one launch (start us, length us, event | category | flops | bytes accessed | tf_op | source)
XLA Modules:
  0.0 328.9 jit_solution(2411669421259678028)
XLA Ops:
  0.8 0.9 copy.25
  1.7 2.8 gather_fusion.1
  5.8 2.8 gather_fusion
  9.0 12.9 %collective-permute-start.1 = (f32[19,1024]{1,0:T(8,128)S(1)}, f32[19,1024]{1,0:T(8,128)S(1)}, u32[]{:S(2)}, u32[]{:S(2)}) collective-permute-start(f32[19,1024]{1,0:T(8,128)S(1)} %pad_maximum_fusion.1), channel_id=1, source_target_pairs={{1,0},{2,1},{3,2},{4,3},{5,4},{6,5},{7,6},{8,7},{9,8},{10,9},{11,1... | collective-permute-start | bytes 233480 | tf_op jit(solution)/shard_map/ppermute | solution.py:21
  21.9 1.9 collective-permute-start
  24.6 27.1 %all_gather.10 = f32[3,8192]{1,0:T(4,128)S(1)} all-gather(f32[3,256]{1,0:T(4,128)S(1)} %copy-done), channel_id=1, replica_groups=mesh['grp'=16,'dev'=32] {'dev'}, dimensions={1}, use_global_device_ids=true | all-gather | bytes 101376 | tf_op jit(solution)/shard_map/all_gather | solution.py:102
  52.8 1.6 while.85
  54.5 1.7 while.86
  56.2 30.2 %all_gather.9 = f32[16,8192]{1,0:T(8,128)S(1)} all-gather(f32[16,256]{1,0:T(8,128)S(1)} %reduce_sum.9), channel_id=1, replica_groups=mesh['grp'=16,'dev'=32] {'dev'}, dimensions={1}, use_global_device_ids=true | all-gather | bytes 540672 | tf_op jit(solution)/shard_map/all_gather | solution.py:101
  88.3 90.3 %psum.7 = f32[16,256]{1,0:T(8,128)S(1)} all-reduce(f32[16,256]{1,0:T(8,128)S(1)} %convolution_multiply_fusion.7), channel_id=1, replica_groups=mesh['grp'=16,'dev'=32] {'dev'}, use_global_device_ids=true, to_apply=%region_7.8 | all-reduce | flops 4096 | bytes 32768 | tf_op jit(solution)/shard_map/psum | solution.py:89
  178.7 24.5 %all_gather.11 = f32[16,4096]{1,0:T(8,128)S(1)} all-gather(f32[16,256]{1,0:T(8,128)S(1)} %psum.7), channel_id=1, replica_groups=mesh['grp'=16,'dev'=32] {'grp'}, dimensions={1}, use_global_device_ids=true | all-gather | bytes 278528 | tf_op jit(solution)/shard_map/all_gather | solution.py:92
  203.1 21.3 %while.91 = (s32[]{:T(128)}, f32[16,256]{1,0:T(8,128)S(1)}, f32[16,4096]{1,0:T(8,128)S(1)}, f32[3,4096]{1,0:T(4,128)}, f32[3,256]{1,0:T(4,128)S(1)}, /*index=5*/...) while((s32[]{:T(128)}, f32[16,256]{1,0:T(8,128)S(1)}, ...), condition=%wide.region_9.10_spmd.clone, body=%wide.region_8.9_spmd.clone.sunk | while | flops 13250586 | bytes 68032 | solution.py:57
  203.1 0.9 constant_dynamic-slice_fusion.38
  204.5 0.9 constant_dynamic-slice_fusion.38
  205.8 0.9 constant_dynamic-slice_fusion.38
  207.1 0.9 constant_dynamic-slice_fusion.38
  208.5 0.9 constant_dynamic-slice_fusion.38
  209.8 0.9 constant_dynamic-slice_fusion.38
  211.1 0.9 constant_dynamic-slice_fusion.38
  212.5 0.9 constant_dynamic-slice_fusion.38
  213.8 0.9 constant_dynamic-slice_fusion.38
  215.1 0.9 constant_dynamic-slice_fusion.38
  216.5 0.9 constant_dynamic-slice_fusion.38
  217.8 0.9 constant_dynamic-slice_fusion.38
  221.8 0.9 constant_dynamic-slice_fusion.38
  224.4 17.1 %while.90 = (s32[]{:T(128)}, f32[16,256]{1,0:T(8,128)S(1)}, f32[16,8192]{1,0:T(8,128)S(1)}, f32[3,8192]{1,0:T(4,128)S(1)}, f32[3,256]{1,0:T(4,128)S(1)}, /*index...) while((s32[]{:T(128)}, f32[16,256]{1,0:T(8,128)S(1)}, ...), condition=%wide.region_6.7_spmd.clone, body=%wide.region_5.6_spmd.clone.sunk | while | flops 13250586 | bytes 68032 | solution.py:57
  241.9 1.8 while.87
  244.7 83.6 %while.89 = (s32[]{:T(128)}, f32[4,16,256]{2,1,0:T(8,128)S(1)}, f32[4,16,256]{2,1,0:T(8,128)S(1)}, f32[4,3,256]{2,1,0:T(4,128)S(1)}, f32[4,16,256]{2,1,0:T(8,128...) while((s32[]{:T(128)}, f32[4,16,256]{2,1,0:T(8,128)S(1)}, ...), condition=%wide.region_15.16_spmd, body=%wide.region_12.15_spmd.sunk | while | flops 39735312 | bytes 213682 | solution.py:131
  246.8 18.8 %while.92 = (s32[]{:T(128)}, f32[16,256]{1,0:T(8,128)S(1)}, s32[]{:T(128)}, s32[8]{0:T(128)S(1)}, s32[]{:T(128)}, /*index=5*/f32[12,19,256]{2,1,0:T(8,128)S(1)},...) while((s32[]{:T(128)}, f32[16,256]{1,0:T(8,128)S(1)}, ...), condition=%wide.region_14.14_spmd, body=%wide.region_13.13_spmd.sunk | while | flops 13250570 | bytes 67841 | solution.py:129
  267.6 18.8 %while.92 = (s32[]{:T(128)}, f32[16,256]{1,0:T(8,128)S(1)}, s32[]{:T(128)}, s32[8]{0:T(128)S(1)}, s32[]{:T(128)}, /*index=5*/f32[12,19,256]{2,1,0:T(8,128)S(1)},...) while((s32[]{:T(128)}, f32[16,256]{1,0:T(8,128)S(1)}, ...), condition=%wide.region_14.14_spmd, body=%wide.region_13.13_spmd.sunk | while | flops 13250570 | bytes 67841 | solution.py:129
  288.5 18.8 %while.92 = (s32[]{:T(128)}, f32[16,256]{1,0:T(8,128)S(1)}, s32[]{:T(128)}, s32[8]{0:T(128)S(1)}, s32[]{:T(128)}, /*index=5*/f32[12,19,256]{2,1,0:T(8,128)S(1)},...) while((s32[]{:T(128)}, f32[16,256]{1,0:T(8,128)S(1)}, ...), condition=%wide.region_14.14_spmd, body=%wide.region_13.13_spmd.sunk | while | flops 13250570 | bytes 67841 | solution.py:129
  309.4 18.8 %while.92 = (s32[]{:T(128)}, f32[16,256]{1,0:T(8,128)S(1)}, s32[]{:T(128)}, s32[8]{0:T(128)S(1)}, s32[]{:T(128)}, /*index=5*/f32[12,19,256]{2,1,0:T(8,128)S(1)},...) while((s32[]{:T(128)}, f32[16,256]{1,0:T(8,128)S(1)}, ...), condition=%wide.region_14.14_spmd, body=%wide.region_13.13_spmd.sunk | while | flops 13250570 | bytes 67841 | solution.py:129
  (312 shorter events, 78.5 us)
Async XLA Ops:
  0.0 0.8 copy-start.3
  4.7 0.8 copy-start.2
  9.0 234.7 %collective-permute-start.1 = (f32[19,1024]{1,0:T(8,128)S(1)}, f32[19,1024]{1,0:T(8,128)S(1)}, u32[]{:S(2)}, u32[]{:S(2)}) collective-permute-start(f32[19,1024]{1,0:T(8,128)S(1)} %pad_maximum_fusion.1), channel_id=1, source_target_pairs={{1,0},{2,1},{3,2},{4,3},{5,4},{6,5},{7,6},{8,7},{9,8},{10,9},{11,1... | collective-permute-start | bytes 233480 | tf_op jit(solution)/shard_map/ppermute | solution.py:21
  21.9 221.8 %collective-permute-start = (f32[19,1024]{1,0:T(8,128)S(1)}, f32[19,1024]{1,0:T(8,128)S(1)}, u32[]{:S(2)}, u32[]{:S(2)}) collective-permute-start(f32[19,1024]{1,0:T(8,128)S(1)} %pad_maximum_fusion.1), channel_id=1, source_target_pairs={{0,1},{1,2},{2,3},{3,4},{4,5},{5,6},{6,7},{7,8},{8,9},{9,10},{10,1... | collective-permute-start | bytes 233480 | tf_op jit(solution)/shard_map/ppermute | solution.py:19
  23.9 0.7 copy-start
  52.1 0.7 copy-start.1
  244.0 0.7 copy-start.4
where the time goes:
time: 331 us; the launch traced here: 329 us
  blocking collectives  172 us (52%)
  local copies, waits for them, and re-layouts  55.4 us (17%)
  loops' own time  45.1 us (14%)
  matrix products  39.9 us (12%)
  starting transfers between devices  14.8 us (4%)
    psum x1, blocking collectives, body(): group_weights = lax.psum(raised, 'dev')  90.3 us
    another operation x4, loops' own time, near_leaf(): return lax.fori_loop(0, slot_total, one_slot, direct)  41.7 us
    dot_general x102, matrix products, translate(): jnp.dot(values, kernel_tile(source, target), precision=lax.Precision.HIGH...  39.9 us
    all_gather x1, blocking collectives, body(): lax.all_gather(block_weights, 'dev', axis=1, tiled=True)  30.2 us
    all_gather x1, blocking collectives, body(): lax.all_gather(skel_block, 'dev', axis=1, tiled=True)  27.1 us
    all_gather x1, blocking collectives, body(): lax.all_gather(group_weights, 'grp', axis=1, tiled=True)  24.5 us
    dynamic_slice x32, local copies, waits for them, and re-layouts, one_slot(): row_nbr[slot_index] - first_leaf  19.9 us
    slice x138, local copies, waits for them, and re-layouts, kernel_tile(): distance = (source[0][:, None] - target[0][None, :]) ** 2  18.6 us
  transfers between devices with their start and end apart: 2, of which 0 were waited for; matrix products, arithmetic and copies ran while one was open for 13% of the time, Pallas kernels for 0%

commit v1 on v0

--- a/solution.py
+++ b/solution.py
@@ -86,7 +86,7 @@
     raised = translate(block_weights, skel_block, own_group, n_blocks * skel_rank)
     empty = jnp.zeros((vectors, skel_rank), jnp.float32)
     group_terms = (n_groups - 1) * skel_rank
-    group_weights = lax.psum(raised, "dev")
+    group_weights = jnp.sum(lax.all_gather(raised, "dev"), axis=0)
     group_field = far_sum(
         empty,
         lax.all_gather(group_weights, "grp", axis=1, tiled=True),

time: 331 us -> 269 us (0.81)
  the two profiles are of different devices: /device:TPU:8 before, /device:TPU:32 now
where the time goes in v1:
time: 269 us; the launch traced here: 267 us
  blocking collectives  121 us (45%)
  local copies, waits for them, and re-layouts  55.3 us (21%)
  loops' own time  45 us (17%)
  matrix products  39.9 us (15%)
  starting transfers between devices  4.33 us (2%)
    another operation x4, loops' own time, near_leaf(): return lax.fori_loop(0, slot_total, one_slot, direct)  41.7 us
    dot_general x102, matrix products, translate(): jnp.dot(values, kernel_tile(source, target), precision=lax.Precision.HIGH...  39.9 us
    all_gather x1, blocking collectives, body(): lax.all_gather(skel_block, 'dev', axis=1, tiled=True)  36.6 us
    all_gather x1, blocking collectives, body(): group_weights = jnp.sum(lax.all_gather(raised, 'dev'), axis=0)  30.2 us
    all_gather x1, blocking collectives, body(): lax.all_gather(block_weights, 'dev', axis=1, tiled=True)  28.2 us
    all_gather x1, blocking collectives, body(): lax.all_gather(group_weights, 'grp', axis=1, tiled=True)  26.1 us
    dynamic_slice x32, local copies, waits for them, and re-layouts, one_slot(): row_nbr[slot_index] - first_leaf  19.8 us
    slice x138, local copies, waits for them, and re-layouts, kernel_tile(): distance = (source[0][:, None] - target[0][None, :]) ** 2  18.6 us
  transfers between devices with their start and end apart: 2, of which 0 were waited for; matrix products, arithmetic and copies ran while one was open for 16% of the time, Pallas kernels for 0%

profile of v1, /device:TPU:32, one launch (start us, length us, event | category | flops | bytes accessed | tf_op | source)
XLA Modules:
  0.0 267.3 jit_solution(6960082484969145661)
XLA Ops:
  0.8 0.9 copy.25
  1.7 2.8 %gather_fusion.1 = f32[1024,3]{1,0:T(8,128)S(1)} fusion(f32[3,1024]{0,1:T(8,128)S(1)} %copy.25, s32[1024]{0:T(1024)S(1)} %fusion.219), kind=kCustom, calls=%fused_computation.1 | custom fusion | bytes 28672 | tf_op jit(solution)/shard_map/jit(_take)/gather | solution.py:71
  5.8 2.8 %gather_fusion = f32[1024,16]{1,0:T(8,128)S(1)} fusion(f32[16,1024]{0,1:T(8,128)S(1)} %copy.23, s32[1024]{0:T(1024)S(1)} %fusion.219), kind=kCustom, calls=%fused_computation | custom fusion | bytes 135168 | tf_op jit(solution)/shard_map/jit(_take)/gather | solution.py:72
  9.0 1.9 collective-permute-start.1
  10.9 2.4 collective-permute-start
  14.0 36.6 %all_gather.16 = f32[3,8192]{1,0:T(4,128)S(1)} all-gather(f32[3,256]{1,0:T(4,128)S(1)} %copy-done), channel_id=1, replica_groups=mesh['grp'=16,'dev'=32] {'dev'}, dimensions={1}, use_global_device_ids=true | all-gather | bytes 101376 | tf_op jit(solution)/shard_map/all_gather | solution.py:102
  51.8 1.6 while.85
  53.5 1.7 while.86
  55.2 28.2 %all_gather.15 = f32[16,8192]{1,0:T(8,128)S(1)} all-gather(f32[16,256]{1,0:T(8,128)S(1)} %reduce_sum.18), channel_id=1, replica_groups=mesh['grp'=16,'dev'=32] {'dev'}, dimensions={1}, use_global_device_ids=true | all-gather | bytes 540672 | tf_op jit(solution)/shard_map/all_gather | solution.py:101
  83.5 17.0 %while.90 = (s32[]{:T(128)}, f32[16,256]{1,0:T(8,128)S(1)}, f32[16,8192]{1,0:T(8,128)S(1)}, f32[3,8192]{1,0:T(4,128)S(1)}, f32[3,256]{1,0:T(4,128)S(1)}, /*index...) while((s32[]{:T(128)}, f32[16,256]{1,0:T(8,128)S(1)}, ...), condition=%wide.region_6.7_spmd.clone, body=%wide.region_5.6_spmd.clone.sunk | while | flops 13250586 | bytes 68032 | solution.py:57
  102.4 30.2 %all-gather = f32[512,256]{1,0:T(8,128)S(1)} all-gather(f32[16,256]{1,0:T(8,128)S(1)} %convolution_multiply_fusion.7), channel_id=2, replica_groups=mesh['grp'=16,'dev'=32] {'dev'}, dimensions={0}, use_global_device_ids=true | all-gather | bytes 540672 | tf_op jit(solution)/shard_map/all_gather | solution.py:89
  132.6 26.1 %all_gather.19 = f32[16,4096]{1,0:T(8,128)S(1)} all-gather(f32[16,256]{1,0:T(8,128)S(1)} %reduce_sum.19), channel_id=1, replica_groups=mesh['grp'=16,'dev'=32] {'grp'}, dimensions={1}, use_global_device_ids=true | all-gather | bytes 278528 | tf_op jit(solution)/shard_map/all_gather | solution.py:92
  158.7 21.3 %while.91 = (s32[]{:T(128)}, f32[16,256]{1,0:T(8,128)S(1)}, f32[16,4096]{1,0:T(8,128)S(1)}, f32[3,4096]{1,0:T(4,128)}, f32[3,256]{1,0:T(4,128)S(1)}, /*index=5*/...) while((s32[]{:T(128)}, f32[16,256]{1,0:T(8,128)S(1)}, ...), condition=%wide.region_9.10_spmd.clone, body=%wide.region_8.9_spmd.clone.sunk | while | flops 13250586 | bytes 68032 | solution.py:57
  158.7 0.9 constant_dynamic-slice_fusion.38
  160.0 0.9 constant_dynamic-slice_fusion.38
  161.3 0.9 constant_dynamic-slice_fusion.38
  162.7 0.9 constant_dynamic-slice_fusion.38
  164.0 0.9 constant_dynamic-slice_fusion.38
  165.3 0.9 constant_dynamic-slice_fusion.38
  166.7 0.9 constant_dynamic-slice_fusion.38
  168.0 0.9 constant_dynamic-slice_fusion.38
  169.3 0.9 constant_dynamic-slice_fusion.38
  170.7 0.9 constant_dynamic-slice_fusion.38
  173.3 0.9 constant_dynamic-slice_fusion.38
  176.0 0.9 constant_dynamic-slice_fusion.38
  178.7 0.9 constant_dynamic-slice_fusion.38
  180.4 1.8 while.87
  183.1 83.5 %while.89 = (s32[]{:T(128)}, f32[4,16,256]{2,1,0:T(8,128)S(1)}, f32[4,16,256]{2,1,0:T(8,128)S(1)}, f32[4,3,256]{2,1,0:T(4,128)S(1)}, f32[4,16,256]{2,1,0:T(8,128...) while((s32[]{:T(128)}, f32[4,16,256]{2,1,0:T(8,128)S(1)}, ...), condition=%wide.region_15.16_spmd, body=%wide.region_12.15_spmd.sunk | while | flops 39735312 | bytes 213682 | solution.py:131
  185.2 18.8 %while.92 = (s32[]{:T(128)}, f32[16,256]{1,0:T(8,128)S(1)}, s32[]{:T(128)}, s32[8]{0:T(128)S(1)}, s32[]{:T(128)}, /*index=5*/f32[12,19,256]{2,1,0:T(8,128)S(1)},...) while((s32[]{:T(128)}, f32[16,256]{1,0:T(8,128)S(1)}, ...), condition=%wide.region_14.14_spmd, body=%wide.region_13.13_spmd.sunk | while | flops 13250570 | bytes 67841 | solution.py:129
  206.1 18.8 %while.92 = (s32[]{:T(128)}, f32[16,256]{1,0:T(8,128)S(1)}, s32[]{:T(128)}, s32[8]{0:T(128)S(1)}, s32[]{:T(128)}, /*index=5*/f32[12,19,256]{2,1,0:T(8,128)S(1)},...) while((s32[]{:T(128)}, f32[16,256]{1,0:T(8,128)S(1)}, ...), condition=%wide.region_14.14_spmd, body=%wide.region_13.13_spmd.sunk | while | flops 13250570 | bytes 67841 | solution.py:129
  227.0 18.8 %while.92 = (s32[]{:T(128)}, f32[16,256]{1,0:T(8,128)S(1)}, s32[]{:T(128)}, s32[8]{0:T(128)S(1)}, s32[]{:T(128)}, /*index=5*/f32[12,19,256]{2,1,0:T(8,128)S(1)},...) while((s32[]{:T(128)}, f32[16,256]{1,0:T(8,128)S(1)}, ...), condition=%wide.region_14.14_spmd, body=%wide.region_13.13_spmd.sunk | while | flops 13250570 | bytes 67841 | solution.py:129
  247.9 18.8 %while.92 = (s32[]{:T(128)}, f32[16,256]{1,0:T(8,128)S(1)}, s32[]{:T(128)}, s32[8]{0:T(128)S(1)}, s32[]{:T(128)}, /*index=5*/f32[12,19,256]{2,1,0:T(8,128)S(1)},...) while((s32[]{:T(128)}, f32[16,256]{1,0:T(8,128)S(1)}, ...), condition=%wide.region_14.14_spmd, body=%wide.region_13.13_spmd.sunk | while | flops 13250570 | bytes 67841 | solution.py:129
  (313 shorter events, 78.5 us)
Async XLA Ops:
  0.0 0.8 copy-start.3
  4.7 0.8 copy-start.2
  9.0 173.2 %collective-permute-start.1 = (f32[19,1024]{1,0:T(8,128)S(1)}, f32[19,1024]{1,0:T(8,128)S(1)}, u32[]{:S(2)}, u32[]{:S(2)}) collective-permute-start(f32[19,1024]{1,0:T(8,128)S(1)} %pad_maximum_fusion.1), channel_id=1, source_target_pairs={{1,0},{2,1},{3,2},{4,3},{5,4},{6,5},{7,6},{8,7},{9,8},{10,9},{11,1... | collective-permute-start | bytes 233480 | tf_op jit(solution)/shard_map/ppermute | solution.py:21
  10.9 171.3 %collective-permute-start = (f32[19,1024]{1,0:T(8,128)S(1)}, f32[19,1024]{1,0:T(8,128)S(1)}, u32[]{:S(2)}, u32[]{:S(2)}) collective-permute-start(f32[19,1024]{1,0:T(8,128)S(1)} %pad_maximum_fusion.1), channel_id=1, source_target_pairs={{0,1},{1,2},{2,3},{3,4},{4,5},{5,6},{6,7},{7,8},{8,9},{9,10},{10,1... | collective-permute-start | bytes 233480 | tf_op jit(solution)/shard_map/ppermute | solution.py:19
  13.4 0.7 copy-start
  51.1 0.7 copy-start.1
  182.5 0.7 copy-start.4
